TPU v7x, 32 devices: a whole 2x2x4 slice. The times are simulated.
32 devices in a mesh: mem: 8 (over z, y), band: 4 (over x, core).
Axes of the slice: x: 2, y: 2, z: 4, core: 2. Of those that a mesh axis runs over, the one named last changes fastest.
Arguments:
- alpha: bfloat16 [16, 4, 320, 720], P('mem', None, 'band'), may hold values from -6 to 6
- static_ctl: bfloat16 [4, 320, 720], P(None, 'band'), may hold values from -6 to 6
- perturbations: bfloat16 [16, 4, 320, 720], P('mem', None, None, 'band'), may hold values from -6 to 6
- static_std: float32 [4, 320, 720], P(None, None, 'band'), may hold values from 0.5 to 2
- lon_root: bfloat16 [720, 720], replicated, may hold values from -0.11 to 1.11
- lat_root: bfloat16 [320, 320], replicated, may hold values from -0.11 to 1.11
- jacobian: bfloat16 [32, 4, 320, 720], P(None, None, 'mem', 'band'), may hold values from -3 to 3
- obs_count: int32 [320, 720], P('mem', 'band'), may hold values from 1 to 6
- channel_mask: int32 [32, 320, 720], P(None, 'mem', 'band'), may hold values 0 or 1
- channel_error: float32 [32], replicated, may hold values from 1 to 2
- member_weight: int32 [16], replicated, may hold values from 1 to 4
Outputs:
- grad_alpha: float32 [16, 4, 320, 720], P('mem', None, 'band')
- grad_static: float32 [4, 320, 720], P(None, 'band')
All inputs are finite; a program needn't handle non-finite values. No bound on the sum of `channel_mask` on one device may be relied on, other than what follows from the above.
Results may differ from a plain program's by a relative error of at most 0.0055.
Values may be sent and summed in bfloat16 or wider, within the bound.
No kernel may reach another device: no remote copies, remote signals or barrier semaphores. Data moves between devices by JAX's collectives and lax.ppermute only.
A program may use at most 64 MiB of HBM per device.

v0:
```python
import jax
import jax.numpy as jnp
from jax import lax
from jax.sharding import PartitionSpec as P


def shards(
    alpha,
    static_ctl,
    perturbations,
    static_std,
    lon_root,
    lat_root,
    jacobian,
    obs_count,
    channel_mask,
    channel_error,
    member_weight,
):
    members = alpha.shape[0]
    rows = jacobian.shape[2]
    rank = lax.axis_index("mem")
    weights = member_weight.astype(jnp.float32)
    coef = weights / jnp.sqrt(jnp.sum(weights * weights))
    own_coef = lax.dynamic_slice_in_dim(coef, rank * members, members, 0)
    fields = jnp.concatenate([alpha, static_ctl[None]], axis=0)
    along_lon = jnp.dot(fields, lon_root, preferred_element_type=jnp.float32).astype(jnp.bfloat16)
    regrouped = lax.all_to_all(along_lon, "band", split_axis=3, concat_axis=2, tiled=True)
    member_lat = jnp.einsum(
        "ij,msjk->msik", lat_root, regrouped[:members], preferred_element_type=jnp.float32
    )
    own_root = lax.dynamic_slice_in_dim(lat_root, rank * rows, rows, 0)
    own_static = jnp.einsum(
        "ij,sjk->sik", own_root, regrouped[members], preferred_element_type=jnp.float32
    )
    scaled = 0.8 * own_coef
    ensemble_term = jnp.sum(
        scaled[:, None, None, None] * perturbations.astype(jnp.float32) * member_lat, axis=0
    )
    summed = lax.psum(ensemble_term, "mem")
    own_sum = lax.dynamic_slice_in_dim(summed, rank * rows, rows, 1)
    own_std = lax.dynamic_slice_in_dim(static_std, rank * rows, rows, 1)
    increment = own_sum + 0.6 * own_std * own_static
    obs_weight = (
        channel_mask.astype(jnp.float32)
        * obs_count.astype(jnp.float32)[None]
        / (channel_error * channel_error)[:, None, None]
    )
    jac_full = jacobian.astype(jnp.float32)
    radiance = jnp.sum(jac_full * increment[None], axis=1)
    obs_gradient = jnp.sum(jac_full * (obs_weight * radiance)[:, None], axis=0).astype(jnp.bfloat16)
    band_gradient = lax.all_gather(obs_gradient, "mem", axis=1, tiled=True).astype(jnp.float32)
    member_adjoint = (
        scaled[:, None, None, None] * perturbations.astype(jnp.float32) * band_gradient[None]
    ).astype(jnp.bfloat16)
    static_adjoint = (0.6 * static_std * band_gradient).astype(jnp.bfloat16)
    adjoints = jnp.concatenate([member_adjoint, static_adjoint[None]], axis=0)
    back_lat = jnp.einsum(
        "ji,msjk->msik", lat_root, adjoints, preferred_element_type=jnp.float32
    ).astype(jnp.bfloat16)
    returned = lax.all_to_all(back_lat, "band", split_axis=2, concat_axis=3, tiled=True)
    back_lon = jnp.einsum("msil,jl->msij", returned, lon_root, preferred_element_type=jnp.float32)
    grad_alpha = alpha.astype(jnp.float32) + back_lon[:members]
    grad_static = static_ctl.astype(jnp.float32) + back_lon[members]
    return (grad_alpha, grad_static)


def solution(mesh):
    in_specs = (
        P("mem", None, "band", None),
        P(None, "band", None),
        P("mem", None, None, "band"),
        P(None, None, "band"),
        P(),
        P(),
        P(None, None, "mem", "band"),
        P("mem", "band"),
        P(None, "mem", "band"),
        P(),
        P(),
    )
    out_specs = (P("mem", None, "band", None), P(None, "band", None))
    return jax.shard_map(shards, mesh=mesh, in_specs=in_specs, out_specs=out_specs, check_vma=False)
```

profile of v0, /device:TPU:0, one launch (start us, length us, event | category | flops | bytes accessed | tf_op | source)
XLA Modules:
  0.0 232.6 jit_solution(4130602733582369304)
XLA Ops:
  7.2 1.2 copy-done
  8.4 2.7 %convolution_convert_fusion.1 = bf16[3,4,80,720]{3,2,1,0:T(8,128)(2,1)S(1)} fusion(bf16[1,4,80,720]{3,2,1,0:T(8,128)(2,1)} %bitcast.52, bf16[2,4,80,720]{3,2,1,0:T(8,128)(2,1)} %param.11, bf16[720,720]{1,0:T(8,128)(2,1)S(1)} %copy-done), kind=kOutput, calls=%fused_computation.13 | convolution fusion | flops 996710400 | bytes 3801600 | tf_op jit(solution)/shard_map/dot_general | solution.py:27
  11.1 3.3 %copy.28 = bf16[3,4,80,720]{2,1,0,3:T(4,128)(2,1)} copy(bf16[3,4,80,720]{3,2,1,0:T(8,128)(2,1)S(1)} %convolution_convert_fusion.1) | data formatting | bytes 2764800 | tf_op jit(solution)/shard_map/convert_element_type | solution.py:27
  14.4 4.4 %all-to-all-start = ((bf16[3,4,80,720]{2,1,0,3:T(4,128)(2,1)}), bf16[3,4,80,720]{2,1,0,3:T(4,128)(2,1)S(1)}, u32[]{:S(2)}, u32[]{:S(2)}) async-start(bf16[3,4,80,720]{2,1,0,3:T(4,128)(2,1)} %copy.28), calls=%async_computation | async-start | bytes 4423680 | tf_op jit(solution)/shard_map/all_to_all | solution.py:28
  20.1 25.5 %all-to-all-done = bf16[3,4,80,720]{2,1,0,3:T(4,128)(2,1)S(1)} async-done(((bf16[3,4,80,720]{2,1,0,3:T(4,128)(2,1)}), bf16[3,4,80,720]{2,1,0,3:T(4,128)(2,1)S(1)}, u32[]{:S(2)}, u32[]{:S(2)}) %all-to-all-start) | async-done | bytes 1382432 | tf_op jit(solution)/shard_map/all_to_all | solution.py:28
  45.6 3.8 %copy.29 = bf16[3,4,80,4,180]{4,2,3,1,0:T(8,128)(2,1)} copy(bf16[3,4,80,4,180]{2,1,0,4,3:T(4,128)(2,1)S(1)} %bitcast.46) | data formatting | bytes 2764800 | tf_op jit(solution)/shard_map/all_to_all | solution.py:28
  49.4 1.5 slice.21
  51.1 1.4 fusion.2
  52.5 1.5 copy.31
  54.6 1.1 slice.22
  55.7 83.2 %all-reduce.2.cloned.1.call-done = f32[4,320,180]{2,1,0:T(8,128)} async-done(((f32[4,320,180]{2,1,0:T(8,128)}), f32[4,320,180]{2,1,0:T(8,128)}) %all-reduce.2.cloned.1.call-update) | async-done | bytes 921616 | tf_op jit(solution)/shard_map/psum | solution.py:40
  138.9 1.2 fusion.13
  140.1 2.6 %fusion = f32[32,40,180]{2,1,0:T(8,128)S(1)} fusion(bf16[32,4,40,180]{3,2,1,0:T(8,128)(2,1)} %param.17, f32[4,40,180]{2,1,0:T(8,128)S(1)} %fusion.13), kind=kLoop, calls=%fused_computation.2 | loop fusion | flops 2534400 | bytes 2880000 | tf_op jit(solution)/shard_map/reduce_sum | solution.py:50
  143.0 1.5 copy-done.1
  145.2 31.8 %all_gather.3 = bf16[4,320,180]{2,0,1:T(4,128)(2,1)S(1)} all-gather(bf16[4,40,180]{2,0,1:T(4,128)(2,1)S(1)} %copy.34), channel_id=1, replica_groups=mesh['mem'=8,'band'=4] {'mem'}, dimensions={1}, use_global_device_ids=true | all-gather | bytes 518400 | tf_op jit(solution)/shard_map/all_gather | solution.py:52
  178.1 1.0 copy-done.5
  180.0 2.5 %fusion.6 = bf16[3,4,320,180]{2,3,1,0:T(8,128)(2,1)} fusion(bf16[1,4,320,180]{2,3,1,0:T(8,128)(2,1)S(1)} %fusion.20, bf16[2,4,320,180]{2,3,1,0:T(8,128)(2,1)S(1)} %multiply_convert_fusion, bf16[320,320]{1,0:T(8,128)(2,1)S(1)} %copy-done.10), kind=kOutput, calls=%fused_computation.14 | convolution fusion | flops 443750400 | bytes 2969600 | tf_op jit(solution)/shard_map/ji,msjk->msik/dot_general | solution.py:58
  182.6 6.7 %copy.37 = bf16[3,4,320,180]{3,1,0,2:T(4,128)(2,1)S(1)} copy(bf16[3,4,320,180]{2,3,1,0:T(8,128)(2,1)} %fusion.6) | data formatting | bytes 2764800 | tf_op jit(solution)/shard_map/convert_element_type | solution.py:60
  189.2 26.8 %all_to_all.33 = bf16[3,4,320,180]{3,1,0,2:T(4,128)(2,1)S(1)} all-to-all(bf16[3,4,320,180]{3,1,0,2:T(4,128)(2,1)S(1)} %copy.37), channel_id=1, replica_groups=mesh['mem'=8,'band'=4] {'band'}, dimensions={2} | all-to-all | bytes 2764800 | tf_op jit(solution)/shard_map/all_to_all | solution.py:61
  216.3 1.0 copy.39
  217.4 2.5 %all_to_all.30 = bf16[3,4,80,720]{3,2,1,0:T(8,128)(2,1)} reshape(bf16[3,4,80,4,180]{4,3,2,1,0:T(4,128)(2,1)S(1)} %copy.39) | data formatting | bytes 2764800 | tf_op jit(solution)/shard_map/all_to_all | solution.py:61
  219.9 2.8 %fusion.16 = f32[3,4,80,720]{3,2,1,0:T(8,128)S(1)} fusion(bf16[3,4,80,720]{3,2,1,0:T(8,128)(2,1)} %all_to_all.30, bf16[720,720]{1,0:T(8,128)(2,1)S(1)} %copy-done), kind=kOutput, calls=%fused_computation.25 | convolution fusion | flops 995328000 | bytes 5184000 | tf_op jit(solution)/shard_map/msil,jl->msij/dot_general | solution.py:62
  222.7 1.0 fusion.19
  224.2 1.5 slice_add_fusion
  (40 shorter events, 5.2 us)
Async XLA Ops:
  7.2 1.3 copy-start
  14.4 4.4 %copy-start.11 = (s32[16]{0:T(128)S(1)}, s32[16]{0:T(128)}, u32[]{:S(2)}) copy-start(s32[16]{0:T(128)} %param.21) | copy-start | bytes 196
  14.4 31.3 %all-to-all-start = ((bf16[3,4,80,720]{2,1,0,3:T(4,128)(2,1)}), bf16[3,4,80,720]{2,1,0,3:T(4,128)(2,1)S(1)}, u32[]{:S(2)}, u32[]{:S(2)}) async-start(bf16[3,4,80,720]{2,1,0,3:T(4,128)(2,1)} %copy.28), calls=%async_computation | async-start | bytes 4423680 | tf_op jit(solution)/shard_map/all_to_all | solution.py:28
  18.7 120.2 %all-reduce.2.cloned.1.call-start = ((), (), s32[]{:S(2)}) async-start(), calls=%async_computation.2 | async-start | bytes 2621440 | tf_op jit(solution)/shard_map/psum | solution.py:40
  49.4 1.6 copy-start.4
  49.4 1.7 copy-start.9
  52.4 1.6 copy-start.12
  52.4 1.6 copy-start.8
  52.5 1.6 copy-start.2
  140.1 2.7 %copy-start.3 = (s32[32,40,180]{2,1,0:T(8,128)S(1)}, s32[32,40,180]{2,1,0:T(8,128)}, u32[]{:S(2)}) copy-start(s32[32,40,180]{2,1,0:T(8,128)} %param.19) | copy-start | bytes 2764804
  142.8 1.7 copy-start.1
  177.8 1.2 copy-start.5
  179.1 0.9 copy-start.10
  219.9 2.8 %copy-start.7 = (bf16[4,80,720]{2,1,0:T(8,128)(2,1)S(1)}, bf16[4,80,720]{2,1,0:T(8,128)(2,1)}, u32[]{:S(2)}) copy-start(bf16[4,80,720]{2,1,0:T(8,128)(2,1)} %param.12) | copy-start | bytes 1382404
  222.7 1.6 copy-start.6
Sparse Core Ops, SparseCore 0:
  54.1 84.7 all-reduce.1
where the time goes:
time: 233 us
  waiting for transfers between devices  109 us (47%)
  blocking collectives  58.6 us (25%)
  local copies, waits for them, and re-layouts  28 us (12%)
  between operations  15 us (6%)
  matrix products  10.5 us (5%)
  other arithmetic  7.4 us (3%)
  starting transfers between devices  4.37 us (2%)
    psum x1, waiting for transfers between devices, shards(): summed = lax.psum(ensemble_term, 'mem')  83.2 us
    all_gather x1, blocking collectives, shards(): lax.all_gather(obs_gradient, 'mem', axis=1, tiled=True).astype(jnp.float32)  31.8 us
    all_to_all x1, blocking collectives, shards(): lax.all_to_all(back_lat, 'band', split_axis=2, concat_axis=3, tiled=True)  26.8 us
    all_to_all x1, waiting for transfers between devices, shards(): lax.all_to_all(along_lon, 'band', split_axis=3, concat_axis=2, tiled=True)  25.5 us
    convert_element_type x1, local copies, waits for them, and re-layouts, shards(): back_lat = jnp.einsum('ji,msjk->msik', lat_root, adjoints, preferred_elem...  6.66 us
    unnamed x27, local copies, waits for them, and re-layouts  5.19 us
  transfers between devices with their start and end apart: 2, of which 2 were waited for; matrix products, arithmetic and copies ran while one was open for 1% of the time, Pallas kernels for 0%

commit v1 on v0

--- a/solution.py
+++ b/solution.py
@@ -37,7 +37,9 @@
     ensemble_term = jnp.sum(
         scaled[:, None, None, None] * perturbations.astype(jnp.float32) * member_lat, axis=0
     )
-    summed = lax.psum(ensemble_term, "mem")
+    summed = ensemble_term
+    for hop in (1, 2, 4):
+        summed = summed + lax.ppermute(summed, "mem", [(dev, dev ^ hop) for dev in range(8)])
     own_sum = lax.dynamic_slice_in_dim(summed, rank * rows, rows, 1)
     own_std = lax.dynamic_slice_in_dim(static_std, rank * rows, rows, 1)
     increment = own_sum + 0.6 * own_std * own_static

time: 233 us -> 254 us (1.090)
  local copies, waits for them, and re-layouts: 28 us -> 41.6 us
  between operations: 15 us -> 1.52 us
  waiting for transfers between devices: 109 us -> 118 us
  starting transfers between devices: 4.37 us -> 11 us
  other arithmetic: 7.4 us -> 12 us
    ppermute x0 -> x3, waiting for transfers between devices: none -> 92 us  [shards(): lax.ppermute(summed, 'mem', [(dev, dev ^ hop) for dev in range(8)])]
    psum x1 -> x0, waiting for transfers between devices: 83.2 us -> none  [shards(): summed = lax.psum(ensemble_term, 'mem')]
    ppermute x0 -> x3, starting transfers between devices: none -> 6.67 us  [shards(): lax.ppermute(summed, 'mem', [(dev, dev ^ hop) for dev in range(8)])]
    add x0 -> x2, other arithmetic: none -> 4.6 us  [shards(): summed + lax.ppermute(summed, 'mem', [(dev, dev ^ hop) for dev in range(8)])]
    ppermute x0 -> x2, local copies, waits for them, and re-layouts: none -> 4.22 us  [shards(): lax.ppermute(summed, 'mem', [(dev, dev ^ hop) for dev in range(8)])]
    add x0 -> x2, local copies, waits for them, and re-layouts: none -> 4.07 us  [shards(): summed + lax.ppermute(summed, 'mem', [(dev, dev ^ hop) for dev in range(8)])]
    unnamed x27 -> x28, local copies, waits for them, and re-layouts: 5.19 us -> 7.19 us
  transfers between devices with their start and end apart: 2 -> 4, of which waited for: 2 -> 4; matrix products, arithmetic and copies ran while one was open for 1% -> 1% of each run, Pallas kernels for 0% -> 0%
where the time goes in v1:
time: 254 us; the launch traced here: 253 us
  waiting for transfers between devices  118 us (46%)
  blocking collectives  58.4 us (23%)
  local copies, waits for them, and re-layouts  41.6 us (16%)
  other arithmetic  12 us (5%)
  starting transfers between devices  11 us (4%)
  matrix products  10.6 us (4%)
    ppermute x3, waiting for transfers between devices, shards(): lax.ppermute(summed, 'mem', [(dev, dev ^ hop) for dev in range(8)])  92 us
    all_gather x1, blocking collectives, shards(): lax.all_gather(obs_gradient, 'mem', axis=1, tiled=True).astype(jnp.float32)  31.6 us
    all_to_all x1, blocking collectives, shards(): lax.all_to_all(back_lat, 'band', split_axis=2, concat_axis=3, tiled=True)  26.8 us
    all_to_all x1, waiting for transfers between devices, shards(): lax.all_to_all(along_lon, 'band', split_axis=3, concat_axis=2, tiled=True)  25.5 us
    unnamed x28, local copies, waits for them, and re-layouts  7.19 us
    ppermute x3, starting transfers between devices, shards(): lax.ppermute(summed, 'mem', [(dev, dev ^ hop) for dev in range(8)])  6.67 us
    convert_element_type x1, local copies, waits for them, and re-layouts, shards(): back_lat = jnp.einsum('ji,msjk->msik', lat_root, adjoints, preferred_elem...  6.66 us
  transfers between devices with their start and end apart: 4, of which 4 were waited for; matrix products, arithmetic and copies ran while one was open for 1% of the time, Pallas kernels for 0%

profile of v1, /device:TPU:0, one launch (start us, length us, event | category | flops | bytes accessed | tf_op | source)
XLA Modules:
  0.0 252.7 jit_solution(177409859315027814)
XLA Ops:
  1.9 2.7 %convolution_convert_fusion.1 = bf16[3,4,80,720]{3,2,1,0:T(8,128)(2,1)S(1)} fusion(bf16[1,4,80,720]{3,2,1,0:T(8,128)(2,1)} %bitcast.54, bf16[2,4,80,720]{3,2,1,0:T(8,128)(2,1)} %param.11, bf16[720,720]{1,0:T(8,128)(2,1)S(1)} %copy-done), kind=kOutput, calls=%fused_computation.13 | convolution fusion | flops 996710400 | bytes 3801600 | tf_op jit(solution)/shard_map/dot_general | solution.py:27
  4.6 3.2 %copy.28 = bf16[3,4,80,720]{2,1,0,3:T(4,128)(2,1)} copy(bf16[3,4,80,720]{3,2,1,0:T(8,128)(2,1)S(1)} %convolution_convert_fusion.1) | data formatting | bytes 2764800 | tf_op jit(solution)/shard_map/convert_element_type | solution.py:27
  7.8 4.4 %all-to-all-start = ((bf16[3,4,80,720]{2,1,0,3:T(4,128)(2,1)}), bf16[3,4,80,720]{2,1,0,3:T(4,128)(2,1)S(1)}, u32[]{:S(2)}, u32[]{:S(2)}) async-start(bf16[3,4,80,720]{2,1,0,3:T(4,128)(2,1)} %copy.28), calls=%async_computation | async-start | bytes 4423680 | tf_op jit(solution)/shard_map/all_to_all | solution.py:28
  13.6 25.5 %all-to-all-done = bf16[3,4,80,720]{2,1,0,3:T(4,128)(2,1)S(1)} async-done(((bf16[3,4,80,720]{2,1,0,3:T(4,128)(2,1)}), bf16[3,4,80,720]{2,1,0,3:T(4,128)(2,1)S(1)}, u32[]{:S(2)}, u32[]{:S(2)}) %all-to-all-start) | async-done | bytes 1382432 | tf_op jit(solution)/shard_map/all_to_all | solution.py:28
  39.1 3.8 %copy.29 = bf16[3,4,80,4,180]{4,2,3,1,0:T(8,128)(2,1)} copy(bf16[3,4,80,4,180]{2,1,0,4,3:T(4,128)(2,1)S(1)} %bitcast.48) | data formatting | bytes 2764800 | tf_op jit(solution)/shard_map/all_to_all | solution.py:28
  47.2 2.3 collective-permute-start
  51.0 22.8 %collective-permute-done = f32[4,320,180]{1,0,2:T(4,128)S(1)} collective-permute-done((f32[4,320,180]{1,0,2:T(4,128)}, f32[4,320,180]{1,0,2:T(4,128)S(1)}, u32[]{:S(2)}, u32[]{:S(2)}) %collective-permute-start) | collective-permute-done | bytes 921632 | tf_op jit(solution)/shard_map/ppermute | solution.py:42
  73.8 2.1 copy.33
  75.9 1.9 add.27
  79.4 1.8 collective-permute-start.1
  81.2 23.7 %collective-permute-done.1 = f32[4,320,180]{1,0,2:T(4,128)S(1)} collective-permute-done((f32[4,320,180]{1,0,2:T(4,128)}, f32[4,320,180]{1,0,2:T(4,128)S(1)}, u32[]{:S(2)}, u32[]{:S(2)}) %collective-permute-start.1) | collective-permute-done | bytes 921632 | tf_op jit(solution)/shard_map/ppermute | solution.py:42
  104.9 2.1 copy.35
  107.0 2.7 %add.28 = f32[4,320,180]{2,1,0:T(8,128)} add(f32[4,320,180]{2,1,0:T(8,128)S(1)} %add.27, f32[4,320,180]{2,1,0:T(8,128)} %copy.35) | non-fusion elementwise | flops 230400 | bytes 2764800 | tf_op jit(solution)/shard_map/add | solution.py:42
  109.7 2.4 copy.36
  112.2 2.5 %collective-permute-start.2 = (f32[4,320,180]{1,0,2:T(4,128)}, f32[4,320,180]{1,0,2:T(4,128)}, u32[]{:S(2)}, u32[]{:S(2)}) collective-permute-start(f32[4,320,180]{1,0,2:T(4,128)} %copy.36), channel_id=1, source_target_pairs={{0,16},{4,20},{8,24},{12,28},{16,0},{20,4},{24,8},{28,12},{1,17},{... | collective-permute-start | bytes 2764808 | tf_op jit(solution)/shard_map/ppermute | solution.py:42
  115.9 45.6 %collective-permute-done.2 = f32[4,320,180]{1,0,2:T(4,128)} collective-permute-done((f32[4,320,180]{1,0,2:T(4,128)}, f32[4,320,180]{1,0,2:T(4,128)}, u32[]{:S(2)}, u32[]{:S(2)}) %collective-permute-start.2) | collective-permute-done | bytes 921632 | tf_op jit(solution)/shard_map/ppermute | solution.py:42
  161.5 2.3 constant_dynamic-slice_fusion
  167.1 2.6 %fusion = f32[32,40,180]{2,1,0:T(8,128)S(1)} fusion(bf16[32,4,40,180]{3,2,1,0:T(8,128)(2,1)} %param.17, f32[4,40,180]{2,1,0:T(8,128)S(1)} %fusion.22), kind=kLoop, calls=%fused_computation.2 | loop fusion | flops 2534400 | bytes 2880000 | tf_op jit(solution)/shard_map/reduce_sum | solution.py:52
  172.2 31.6 %all_gather.3 = bf16[4,320,180]{2,0,1:T(4,128)(2,1)S(1)} all-gather(bf16[4,40,180]{2,0,1:T(4,128)(2,1)S(1)} %copy.40), channel_id=1, replica_groups=mesh['mem'=8,'band'=4] {'mem'}, dimensions={1}, use_global_device_ids=true | all-gather | bytes 518400 | tf_op jit(solution)/shard_map/all_gather | solution.py:54
  207.0 2.5 %fusion.6 = bf16[3,4,320,180]{2,3,1,0:T(8,128)(2,1)} fusion(bf16[1,4,320,180]{2,3,1,0:T(8,128)(2,1)S(1)} %fusion.19, bf16[2,4,320,180]{2,3,1,0:T(8,128)(2,1)S(1)} %multiply_convert_fusion, bf16[320,320]{1,0:T(8,128)(2,1)S(1)} %copy-done.10), kind=kOutput, calls=%fused_computation.14 | convolution fusion | flops 443750400 | bytes 2969600 | tf_op jit(solution)/shard_map/ji,msjk->msik/dot_general | solution.py:60
  209.5 6.7 %copy.43 = bf16[3,4,320,180]{3,1,0,2:T(4,128)(2,1)S(1)} copy(bf16[3,4,320,180]{2,3,1,0:T(8,128)(2,1)} %fusion.6) | data formatting | bytes 2764800 | tf_op jit(solution)/shard_map/convert_element_type | solution.py:62
  216.2 26.8 %all_to_all.33 = bf16[3,4,320,180]{3,1,0,2:T(4,128)(2,1)S(1)} all-to-all(bf16[3,4,320,180]{3,1,0,2:T(4,128)(2,1)S(1)} %copy.43), channel_id=1, replica_groups=mesh['mem'=8,'band'=4] {'band'}, dimensions={2} | all-to-all | bytes 2764800 | tf_op jit(solution)/shard_map/all_to_all | solution.py:63
  244.3 2.5 all_to_all.30
  246.9 2.8 %fusion.15 = f32[3,4,80,720]{3,2,1,0:T(8,128)S(1)} fusion(bf16[3,4,80,720]{3,2,1,0:T(8,128)(2,1)} %all_to_all.30, bf16[720,720]{1,0:T(8,128)(2,1)S(1)} %copy-done), kind=kOutput, calls=%fused_computation.24 | convolution fusion | flops 995328000 | bytes 5184000 | tf_op jit(solution)/shard_map/msil,jl->msij/dot_general | solution.py:64
  (51 shorter events, 23.8 us)
Async XLA Ops:
  0.6 1.3 copy-start
  7.8 4.4 %copy-start.11 = (s32[16]{0:T(128)S(1)}, s32[16]{0:T(128)}, u32[]{:S(2)}) copy-start(s32[16]{0:T(128)} %param.21) | copy-start | bytes 196
  7.8 31.3 %all-to-all-start = ((bf16[3,4,80,720]{2,1,0,3:T(4,128)(2,1)}), bf16[3,4,80,720]{2,1,0,3:T(4,128)(2,1)S(1)}, u32[]{:S(2)}, u32[]{:S(2)}) async-start(bf16[3,4,80,720]{2,1,0,3:T(4,128)(2,1)} %copy.28), calls=%async_computation | async-start | bytes 4423680 | tf_op jit(solution)/shard_map/all_to_all | solution.py:28
  42.8 1.6 copy-start.4
  42.8 1.7 copy-start.9
  47.2 26.6 %collective-permute-start = (f32[4,320,180]{1,0,2:T(4,128)}, f32[4,320,180]{1,0,2:T(4,128)S(1)}, u32[]{:S(2)}, u32[]{:S(2)}) collective-permute-start(f32[4,320,180]{1,0,2:T(4,128)} %copy.31), channel_id=1, source_target_pairs={{0,4},{4,0},{8,12},{12,8},{16,20},{20,16},{24,28},{28,24},{1,5},{5... | collective-permute-start | bytes 2764808 | tf_op jit(solution)/shard_map/ppermute | solution.py:42
  79.4 25.5 %collective-permute-start.1 = (f32[4,320,180]{1,0,2:T(4,128)}, f32[4,320,180]{1,0,2:T(4,128)S(1)}, u32[]{:S(2)}, u32[]{:S(2)}) collective-permute-start(f32[4,320,180]{1,0,2:T(4,128)} %copy.34), channel_id=1, source_target_pairs={{0,8},{4,12},{8,0},{12,4},{16,24},{20,28},{24,16},{28,20},{1,9},{5... | collective-permute-start | bytes 2764808 | tf_op jit(solution)/shard_map/ppermute | solution.py:42
  109.7 5.0 %copy-start.12 = (f32[32]{0:T(128)S(1)}, f32[32]{0:T(128)}, u32[]{:S(2)}) copy-start(f32[32]{0:T(128)} %param.20) | copy-start | bytes 388
  109.7 5.0 %copy-start.8 = (s32[40,180]{1,0:T(8,128)S(1)}, s32[40,180]{1,0:T(8,128)}, u32[]{:S(2)}) copy-start(s32[40,180]{1,0:T(8,128)} %param.18) | copy-start | bytes 86404
  109.7 51.8 %copy-start.2 = (f32[4,320,180]{1,0,2:T(4,128)S(1)}, f32[4,320,180]{1,0,2:T(4,128)}, u32[]{:S(2)}) copy-start(f32[4,320,180]{1,0,2:T(4,128)} %param.14) | copy-start | bytes 2764804
  112.2 49.3 %collective-permute-start.2 = (f32[4,320,180]{1,0,2:T(4,128)}, f32[4,320,180]{1,0,2:T(4,128)}, u32[]{:S(2)}, u32[]{:S(2)}) collective-permute-start(f32[4,320,180]{1,0,2:T(4,128)} %copy.36), channel_id=1, source_target_pairs={{0,16},{4,20},{8,24},{12,28},{16,0},{20,4},{24,8},{28,12},{1,17},{... | collective-permute-start | bytes 2764808 | tf_op jit(solution)/shard_map/ppermute | solution.py:42
  167.0 2.7 %copy-start.3 = (s32[32,40,180]{2,1,0:T(8,128)S(1)}, s32[32,40,180]{2,1,0:T(8,128)}, u32[]{:S(2)}) copy-start(s32[32,40,180]{2,1,0:T(8,128)} %param.19) | copy-start | bytes 2764804
  169.7 1.7 copy-start.1
  204.8 1.2 copy-start.5
  206.1 0.9 copy-start.10
  246.9 2.8 %copy-start.7 = (bf16[4,80,720]{2,1,0:T(8,128)(2,1)S(1)}, bf16[4,80,720]{2,1,0:T(8,128)(2,1)}, u32[]{:S(2)}) copy-start(bf16[4,80,720]{2,1,0:T(8,128)(2,1)} %param.12) | copy-start | bytes 1382404
  249.7 1.6 copy-start.6
